TPU v7x, 32 devices: a whole 2x2x4 slice. The times are simulated.
32 devices in a mesh: tm: 16 (over z, y, x), seq: 2 (over core).
Axes of the slice: x: 2, y: 2, z: 4, core: 2. Of those that a mesh axis runs over, the one named last changes fastest.
Arguments:
- gains: float32 [128, 128, 128], P(('seq', 'tm')), parts along dimension 0, may hold values from -1 to 1
- offsets: float32 [128, 128], P(('seq', 'tm')), parts along dimension 0, may hold values from -8 to 8
- cov_terms: float32 [128, 128, 128], P(('seq', 'tm')), parts along dimension 0, as said below
Outputs:
- smoothed_means: float32 [128, 128], P(('seq', 'tm')), parts along dimension 0
- smoothed_covs: float32 [128, 128, 128], P(('seq', 'tm')), parts along dimension 0
- moments: float32 [256, 128], P('seq'), parts along dimension 0
There are 2 independent parts, one for each index of `seq`. A program takes and returns all parts, laid end to end along the dimension named above; each array names one. Nothing has to cross between parts.
Inputs may be any that keep to these rules, and one draw needn't show every extreme that they name: `cov_terms`: each step's covariance term is symmetric positive definite.
All inputs are finite; a program needn't handle non-finite values.
Results may differ from a plain program's by a relative error of at most 0.00014.
Values sent between devices are 32-bit elements; how exact they have to be, the bound alone decides.
A program may use at most 128 MiB of HBM per device.

v0:
```python
import jax
import jax.numpy as jnp
from jax import lax
from jax.sharding import PartitionSpec as P


def prefix(part, axis, combine, identity):
    count = lax.axis_size(axis)
    place = lax.axis_index(axis)
    ahead = count - 1 - place
    gathered = jax.tree.map(lambda a: lax.all_gather(a, axis), part)
    state = jax.tree.map(lambda a, e: jnp.zeros_like(a) + jnp.asarray(e, a.dtype), part, identity)

    def one(lap, state):
        source = count - 1 - lap
        return combine(
            state, jax.tree.map(lambda a: lax.dynamic_index_in_dim(a, source, 0, False), gathered)
        )

    return lax.fori_loop(0, ahead, one, state)


def product(left, right):
    return jnp.dot(left, right, precision=lax.Precision.HIGHEST, preferred_element_type=jnp.float32)


def compose(earlier, following):
    gain_left, offset_left, prior_spread_matrix = earlier
    gain_right, offset_right, cov_right = following
    gain = product(gain_left, gain_right)
    offset = offset_left + product(gain_left, offset_right)
    covariance = prior_spread_matrix + product(product(gain_left, cov_right), gain_left.T)
    return (gain, offset, covariance)


def join_higher(higher, lower):
    return compose(lower, higher)


def drop_suffix(boundary, element):
    merged = compose(element, boundary)
    return (merged, None)


def walk(state_pair, element):
    upcoming_average, cov_next = state_pair
    gain, offset, covariance = element
    mean_now = offset + product(gain, upcoming_average)
    cov_now = covariance + product(product(gain, cov_next), gain.T)
    return ((mean_now, cov_now), (mean_now, cov_now))


def local(gains, offsets, cov_terms):
    devices = lax.axis_size("tm")
    position = lax.axis_index("tm")
    local_steps = gains.shape[0]
    width = gains.shape[1]
    final_step = jnp.logical_and(
        jnp.arange(local_steps) == local_steps - 1, position == devices - 1
    )
    gains = jnp.where(final_step[:, None, None], jnp.zeros_like(gains), gains)
    unit = (
        jnp.eye(width, dtype=jnp.float32),
        jnp.zeros((width,), jnp.float32),
        jnp.zeros((width, width), jnp.float32),
    )
    aggregate, unused = lax.scan(drop_suffix, unit, (gains, offsets, cov_terms), reverse=True)
    boundary = prefix((aggregate[0], aggregate[1], aggregate[2]), "tm", join_higher, unit)
    final_pair, outputs = lax.scan(
        walk, (boundary[1], boundary[2]), (gains, offsets, cov_terms), reverse=True
    )
    mean_rows, cov_rows = outputs
    local_moment = jnp.sum(cov_rows, axis=0) + product(mean_rows.T, mean_rows)
    total_moment = lax.psum(local_moment, "tm")
    moments = total_moment / (local_steps * devices)
    return (mean_rows, cov_rows, moments)


def solution(mesh):
    in_specs = (P(("seq", "tm"), None, None), P(("seq", "tm"), None), P(("seq", "tm"), None, None))
    out_specs = (P(("seq", "tm"), None), P(("seq", "tm"), None, None), P("seq", None))
    return jax.shard_map(local, mesh=mesh, in_specs=in_specs, out_specs=out_specs, check_vma=False)
```

profile of v0, /device:TPU:0, one launch (start us, length us, event | category | flops | bytes accessed | tf_op | source)
XLA Modules:
  0.0 288.2 jit_solution(3906093262499196804)
XLA Ops:
  8.4 3.9 %while.57 = (s32[]{:T(128)}, f32[128,128]{1,0:T(8,128)S(1)}, f32[128]{0:T(128)S(1)}, f32[128,128]{1,0:T(8,128)S(1)}, f32[4,128,128]{2,1,0:T(8,128)S(1)}, /*index...) while((s32[]{:T(128)}, f32[128,128]{1,0:T(8,128)S(1)}, ...), condition=%wide.region_1.2_spmd.clone, body=%wide.region_0.1_spmd.clone.sunk | while | flops 75727104 | bytes 857219 | solution.py:67
  13.7 42.2 %all-gather.3 = f32[16,1,128]{2,1,0:T(1,128)S(1)} all-gather(f32[1,1,128]{2,1,0:T(1,128)S(1)} %bitcast.141), channel_id=2, replica_groups=mesh['tm'=16,'seq'=2] {'tm'}, dimensions={0}, use_global_device_ids=true | all-gather | bytes 8704 | tf_op jit(solution)/shard_map/all_gather | solution.py:11
  55.9 15.2 %all-gather.7.cloned.1.call-done = f32[2048,128]{1,0:T(8,128)} async-done(((f32[128,128]{1,0:T(8,128)}), f32[2048,128]{1,0:T(8,128)}) %all-gather.7.cloned.1.call-update) | async-done | bytes 1048592 | tf_op jit(solution)/shard_map/all_gather | solution.py:11
  71.1 57.4 %all-gather.9.cloned.1.call-done = f32[2048,128]{1,0:T(8,128)} async-done(((f32[128,128]{1,0:T(8,128)}), f32[2048,128]{1,0:T(8,128)}) %all-gather.9.cloned.1.call-update) | async-done | bytes 1048592 | tf_op jit(solution)/shard_map/all_gather | solution.py:11
  128.5 49.0 %while.55 = (s32[]{:T(128)}, f32[128]{0:T(128)S(1)}, f32[128,128]{1,0:T(8,128)S(1)}, s32[]{:T(128)}, f32[16,128]{1,0:T(8,128)S(1)}, /*index=5*/f32[16,128,128]{2...) while((s32[]{:T(128)}, f32[128]{0:T(128)S(1)}, ...), condition=%wide.region_3.4_spmd, body=%wide.region_2.3_spmd.sunk | while | flops 50544772 | bytes 529055 | solution.py:20
  129.6 1.1 convolution_add_fusion.6
  132.8 1.1 convolution_add_fusion.6
  136.1 1.1 convolution_add_fusion.6
  139.4 1.1 convolution_add_fusion.6
  142.7 1.1 convolution_add_fusion.6
  145.9 1.1 convolution_add_fusion.6
  149.2 1.1 convolution_add_fusion.6
  152.5 1.1 convolution_add_fusion.6
  155.7 1.1 convolution_add_fusion.6
  159.0 1.1 convolution_add_fusion.6
  162.3 1.1 convolution_add_fusion.6
  164.5 1.1 fusion.92
  165.6 1.1 convolution_add_fusion.6
  168.8 1.1 convolution_add_fusion.6
  172.1 1.1 convolution_add_fusion.6
  175.4 1.1 convolution_add_fusion.6
  177.6 3.0 %while.56 = (s32[]{:T(128)}, f32[128]{0:T(128)S(1)}, f32[128,128]{1,0:T(8,128)S(1)}, f32[4,128]{1,0:T(4,128)S(1)}, f32[4,128,128]{2,1,0:T(8,128)S(1)}, /*index=5...) while((s32[]{:T(128)}, f32[128]{0:T(128)S(1)}, ...), condition=%wide.region_5.6_spmd, body=%wide.region_4.5_spmd.sunk | while | flops 50544768 | bytes 595585 | solution.py:69
  182.2 98.0 %all-reduce.2.cloned.1.call-done = f32[128,128]{1,0:T(8,128)} async-done(((f32[128,128]{1,0:T(8,128)}), f32[128,128]{1,0:T(8,128)}) %all-reduce.2.cloned.1.call-update) | async-done | bytes 65552 | tf_op jit(solution)/shard_map/psum | solution.py:74
  280.2 1.5 broadcast_multiply_fusion
  (117 shorter events, 41.2 us)
Async XLA Ops:
  7.2 63.9 %all-gather.7.cloned.1.call-start = ((), (), s32[]{:S(2)}) async-start(), calls=%async_computation.1 | async-start | bytes 1114112 | tf_op jit(solution)/shard_map/all_gather | solution.py:11
  7.3 1.1 copy-start.2
  7.3 1.1 copy-start.5
  12.3 0.6 copy-start
  12.3 0.7 copy-start.1
  12.9 115.6 %all-gather.9.cloned.1.call-start = ((), (), s32[]{:S(2)}) async-start(), calls=%async_computation.2 | async-start | bytes 1114112 | tf_op jit(solution)/shard_map/all_gather | solution.py:11
  13.7 266.5 %all-reduce.2.cloned.1.call-start = ((), (), s32[]{:S(2)}) async-start(), calls=%async_computation | async-start | bytes 131072 | tf_op jit(solution)/shard_map/psum | solution.py:74
  180.7 0.6 copy-start.4
  180.7 1.5 copy-start.3
Sparse Core Ops, SparseCore 0:
  13.0 57.9 all-gather.6
  74.4 54.0 all-gather.8
  182.3 97.8 all-reduce.1
where the time goes:
time: 291 us; the launch traced here: 288 us
  waiting for transfers between devices  171 us (59%)
  matrix products  55.8 us (19%)
  blocking collectives  42.2 us (15%)
  between operations  13.9 us (5%)
    psum x1, waiting for transfers between devices, local(): total_moment = lax.psum(local_moment, 'tm')  98 us
    all_gather x2, waiting for transfers between devices, prefix(): gathered = jax.tree.map(lambda a: lax.all_gather(a, axis), part)  72.6 us
    dot_general x74, matrix products, product(): jnp.dot(left, right, precision=lax.Precision.HIGHEST, preferred_element_t...  55.8 us
    all_gather x1, blocking collectives, prefix(): gathered = jax.tree.map(lambda a: lax.all_gather(a, axis), part)  42.2 us
  transfers between devices with their start and end apart: 3, of which 3 were waited for; matrix products, arithmetic and copies ran while one was open for 0% of the time, Pallas kernels for 0%

commit v1 on v0

--- a/solution.py
+++ b/solution.py
@@ -71,7 +71,7 @@
     )
     mean_rows, cov_rows = outputs
     local_moment = jnp.sum(cov_rows, axis=0) + product(mean_rows.T, mean_rows)
-    total_moment = lax.psum(local_moment, "tm")
+    total_moment = jnp.sum(lax.all_gather(local_moment, "tm"), axis=0)
     moments = total_moment / (local_steps * devices)
     return (mean_rows, cov_rows, moments)
 

time: 291 us -> 244 us (0.84)
  waiting for transfers between devices: 171 us -> 125 us
    psum x1 -> x0, waiting for transfers between devices: 98 us -> none  [local(): total_moment = lax.psum(local_moment, 'tm')]
    all_gather x0 -> x1, waiting for transfers between devices: none -> 51.3 us  [local(): total_moment = jnp.sum(lax.all_gather(local_moment, 'tm'), axis=0)]
where the time goes in v1:
time: 244 us; the launch traced here: 242 us
  waiting for transfers between devices  125 us (51%)
  matrix products  55.8 us (23%)
  blocking collectives  42.2 us (17%)
  between operations  13.9 us (6%)
  other arithmetic  3.04 us (1%)
    all_gather x2, waiting for transfers between devices, prefix(): gathered = jax.tree.map(lambda a: lax.all_gather(a, axis), part)  72.6 us
    dot_general x74, matrix products, product(): jnp.dot(left, right, precision=lax.Precision.HIGHEST, preferred_element_t...  55.8 us
    all_gather x1, waiting for transfers between devices, local(): total_moment = jnp.sum(lax.all_gather(local_moment, 'tm'), axis=0)  51.3 us
    all_gather x1, blocking collectives, prefix(): gathered = jax.tree.map(lambda a: lax.all_gather(a, axis), part)  42.2 us
  transfers between devices with their start and end apart: 3, of which 3 were waited for; matrix products, arithmetic and copies ran while one was open for 0% of the time, Pallas kernels for 0%

profile of v1, /device:TPU:0, one launch (start us, length us, event | category | flops | bytes accessed | tf_op | source)
XLA Modules:
  0.0 241.9 jit_solution(14477430081322075973)
XLA Ops:
  8.4 3.9 %while.57 = (s32[]{:T(128)}, f32[128,128]{1,0:T(8,128)S(1)}, f32[128]{0:T(128)S(1)}, f32[128,128]{1,0:T(8,128)S(1)}, f32[4,128,128]{2,1,0:T(8,128)S(1)}, /*index...) while((s32[]{:T(128)}, f32[128,128]{1,0:T(8,128)S(1)}, ...), condition=%wide.region_1.2_spmd.clone, body=%wide.region_0.1_spmd.clone.sunk | while | flops 75727104 | bytes 857219 | solution.py:67
  13.7 42.2 %all-gather.4 = f32[16,1,128]{2,1,0:T(1,128)S(1)} all-gather(f32[1,1,128]{2,1,0:T(1,128)S(1)} %bitcast.143), channel_id=2, replica_groups=mesh['tm'=16,'seq'=2] {'tm'}, dimensions={0}, use_global_device_ids=true | all-gather | bytes 8704 | tf_op jit(solution)/shard_map/all_gather | solution.py:11
  55.9 15.2 %all-gather.9.cloned.1.call-done = f32[2048,128]{1,0:T(8,128)} async-done(((f32[128,128]{1,0:T(8,128)}), f32[2048,128]{1,0:T(8,128)}) %all-gather.9.cloned.1.call-update) | async-done | bytes 1048592 | tf_op jit(solution)/shard_map/all_gather | solution.py:11
  71.1 57.4 %all-gather.11.cloned.1.call-done = f32[2048,128]{1,0:T(8,128)} async-done(((f32[128,128]{1,0:T(8,128)}), f32[2048,128]{1,0:T(8,128)}) %all-gather.11.cloned.1.call-update) | async-done | bytes 1048592 | tf_op jit(solution)/shard_map/all_gather | solution.py:11
  128.5 49.0 %while.55 = (s32[]{:T(128)}, f32[128]{0:T(128)S(1)}, f32[128,128]{1,0:T(8,128)S(1)}, s32[]{:T(128)}, f32[16,128]{1,0:T(8,128)S(1)}, /*index=5*/f32[16,128,128]{2...) while((s32[]{:T(128)}, f32[128]{0:T(128)S(1)}, ...), condition=%wide.region_3.4_spmd, body=%wide.region_2.3_spmd.sunk | while | flops 50544772 | bytes 529055 | solution.py:20
  129.6 1.1 convolution_add_fusion.6
  132.8 1.1 convolution_add_fusion.6
  136.1 1.1 convolution_add_fusion.6
  139.4 1.1 convolution_add_fusion.6
  142.6 1.1 convolution_add_fusion.6
  145.9 1.1 convolution_add_fusion.6
  149.2 1.1 convolution_add_fusion.6
  152.5 1.1 convolution_add_fusion.6
  155.7 1.1 convolution_add_fusion.6
  159.0 1.1 convolution_add_fusion.6
  162.3 1.1 convolution_add_fusion.6
  165.5 1.1 convolution_add_fusion.6
  168.8 1.1 convolution_add_fusion.6
  171.0 1.1 fusion.92
  172.1 1.1 convolution_add_fusion.6
  175.4 1.1 convolution_add_fusion.6
  177.6 3.0 %while.56 = (s32[]{:T(128)}, f32[128]{0:T(128)S(1)}, f32[128,128]{1,0:T(8,128)S(1)}, f32[4,128]{1,0:T(4,128)S(1)}, f32[4,128,128]{2,1,0:T(8,128)S(1)}, /*index=5...) while((s32[]{:T(128)}, f32[128]{0:T(128)S(1)}, ...), condition=%wide.region_5.6_spmd, body=%wide.region_4.5_spmd.sunk | while | flops 50544768 | bytes 595585 | solution.py:69
  182.2 51.3 %all-gather.13.cloned.1.call-done = f32[2048,128]{1,0:T(8,128)} async-done(((f32[128,128]{1,0:T(8,128)}), f32[2048,128]{1,0:T(8,128)}) %all-gather.13.cloned.1.call-update) | async-done | bytes 1048592 | tf_op jit(solution)/shard_map/all_gather | solution.py:74
  233.5 1.3 reduce_sum.19
  (118 shorter events, 41.9 us)
Async XLA Ops:
  7.2 63.9 %all-gather.9.cloned.1.call-start = ((), (), s32[]{:S(2)}) async-start(), calls=%async_computation | async-start | bytes 1114112 | tf_op jit(solution)/shard_map/all_gather | solution.py:11
  7.3 1.1 copy-start.2
  7.3 1.1 copy-start.5
  12.3 0.6 copy-start
  12.3 0.7 copy-start.1
  12.9 115.6 %all-gather.11.cloned.1.call-start = ((), (), s32[]{:S(2)}) async-start(), calls=%async_computation.1 | async-start | bytes 1114112 | tf_op jit(solution)/shard_map/all_gather | solution.py:11
  13.7 219.8 %all-gather.13.cloned.1.call-start = ((), (), s32[]{:S(2)}) async-start(), calls=%async_computation.2 | async-start | bytes 1114112 | tf_op jit(solution)/shard_map/all_gather | solution.py:74
  180.7 0.6 copy-start.4
  180.7 1.5 copy-start.3
Sparse Core Ops, SparseCore 0:
  13.0 57.9 all-gather.8
  74.4 54.0 all-gather.10
  182.3 51.1 all-gather.12
